TPU v7x, 256 devices: a whole 4x4x8 slice. The times are simulated.
256 devices in a mesh: scen: 16 (over y, x), blk: 16 (over z, core).
Axes of the slice: x: 4, y: 4, z: 8, core: 2. Of those that a mesh axis runs over, the one named last changes fastest.
Arguments:
- link: bfloat16 [64, 256, 4096], P('scen', None, 'blk'), may hold values from -0.15625 to 0.15625
- leaf_inverse: bfloat16 [64, 256, 256], P('scen'), as said below
- leaf_rhs: float32 [64, 256], P('scen'), may hold values from -6 to 6
- node_rhs: float32 [2, 4096], P(None, 'blk'), may hold values from -6 to 6
- node_diag: float32 [2, 4096], P(None, 'blk'), may hold values from 0.5 to 4
- parent: int32 [64], P('scen'), may hold values from 0 to 1
- tile_mask: int32 [64, 16], P('scen', 'blk'), may hold values 0 or 1
Outputs:
- node_solution: float32 [2, 4096], P(None, 'blk')
- leaf_solution: float32 [64, 256], P('scen')
- schur: float32 [2, 4096, 4096], P(None, 'blk', 'scen')
Inputs may be any that keep to these rules, and one draw needn't show every extreme that they name: `leaf_inverse`: its diagonal entries lie within 1 to 2.
All inputs are finite; a program needn't handle non-finite values. No bound on the sum of `tile_mask` on one device may be relied on, other than what follows from the above.
Results may differ from a plain program's by a relative error of at most 0.0017.
Values may be sent and summed in bfloat16 or wider, within the bound.
A program may use at most 128 MiB of HBM per device.

v0:
```python
import jax
import jax.numpy as jnp
from jax import lax
from jax.sharding import PartitionSpec as P

ITERS = 4


highest = lax.Precision.HIGHEST
damping = 0.4


def body(link, leaf_inverse, leaf_rhs, node_rhs, node_diag, parent, tile_mask):
    leaf_count, width_leaf, tile_width = link.shape
    node_count = node_rhs.shape[0]
    scen_count = lax.axis_size("scen")
    blk_count = lax.axis_size("blk")
    full_width = tile_width * blk_count
    scen_index = lax.axis_index("scen")
    blk_index = lax.axis_index("blk")
    node_ids = lax.broadcasted_iota(jnp.int32, (leaf_count, node_count), 1)
    member = parent[:, None] == node_ids
    member_f = member.astype(jnp.float32)
    masked = link * tile_mask.astype(jnp.bfloat16)[:, :, None]
    solved = jnp.einsum(
        "lnm,lmc->lnc", leaf_inverse, masked, preferred_element_type=jnp.float32
    ).astype(jnp.bfloat16)
    chosen = masked[None] * member.astype(jnp.bfloat16).T[:, :, None, None]
    chosen = chosen.reshape(node_count, leaf_count * width_leaf, tile_width)
    portion = lax.all_gather(solved, "blk", axis=2, tiled=True)
    stacked = portion.reshape(leaf_count * width_leaf, portion.shape[2])
    partial_value = jnp.einsum("pkr,kc->prc", chosen, stacked, preferred_element_type=jnp.float32)
    diagonal_tile = lax.dynamic_slice_in_dim(partial_value, blk_index * tile_width, tile_width, 2)
    diag_terms = jnp.diagonal(diagonal_tile, axis1=1, axis2=2)
    inverse_f = leaf_inverse.astype(jnp.float32)
    masked_f = masked.astype(jnp.float32)
    leaf_solve = jnp.einsum("lnm,lm->ln", inverse_f, leaf_rhs, precision=highest)
    leaf_terms = jnp.einsum("lnc,ln->lc", masked_f, leaf_solve, precision=highest)
    rhs_terms = jnp.dot(member_f.T, leaf_terms, precision=highest)
    rhs_sum, diag_sum = lax.psum((rhs_terms, diag_terms), "scen")
    reduced = node_rhs - rhs_sum
    scaling = node_diag + diag_sum
    schur_rows = lax.psum_scatter(partial_value, "scen", scatter_dimension=1, tiled=True)
    schur_out = lax.all_to_all(schur_rows, "scen", split_axis=2, concat_axis=1, tiled=True)
    row_count = schur_rows.shape[1]

    def own_rows(values):
        return lax.dynamic_slice_in_dim(values, scen_index * row_count, row_count, 1)

    reduced_own = own_rows(reduced)
    scaling_own = own_rows(scaling)
    diag_own = own_rows(node_diag)

    def assemble(portion):
        gathered = lax.all_gather(portion, ("scen", "blk"), axis=1, tiled=True)
        gathered = gathered.reshape(node_count, scen_count, blk_count, row_count)
        return gathered.transpose(0, 2, 1, 3).reshape(node_count, full_width)

    portion = reduced_own / scaling_own
    for sweep in range(ITERS):
        entire = assemble(portion)
        product = diag_own * portion + jnp.einsum(
            "prc,pc->pr", schur_rows, entire, precision=highest
        )
        portion = portion + damping * (reduced_own - product) / scaling_own
    node_solution = lax.dynamic_slice_in_dim(
        assemble(portion), blk_index * tile_width, tile_width, 1
    )
    parent_values = jnp.dot(member_f, node_solution, precision=highest)
    link_term = jnp.einsum("lnc,lc->ln", masked_f, parent_values, precision=highest)
    summed = lax.psum(link_term, "blk")
    leaf_solution = jnp.einsum("lnm,lm->ln", inverse_f, leaf_rhs - summed, precision=highest)
    return (node_solution, leaf_solution, schur_out)


def solution(mesh):
    in_specs = (
        P("scen", None, "blk"),
        P("scen", None, None),
        P("scen", None),
        P(None, "blk"),
        P(None, "blk"),
        P("scen"),
        P("scen", "blk"),
    )
    out_specs = (P(None, "blk"), P("scen", None), P(None, "blk", "scen"))
    return jax.shard_map(body, mesh=mesh, in_specs=in_specs, out_specs=out_specs, check_vma=False)
```

profile of v0, /device:TPU:17, one launch (start us, length us, event | category | flops | bytes accessed | tf_op | source)
XLA Modules:
  0.0 512.7 jit_solution(16813011652913458101)
XLA Ops:
  7.2 0.7 convert_bitcast_fusion
  7.9 1.1 broadcast_multiply_fusion
  9.1 1.1 fusion.5
  10.3 0.2 copy.43
  10.5 0.7 compare_convert_fusion
  11.2 58.3 %all-gather.7.cloned.1.call-done = bf16[4,256,4096]{1,2,0:T(8,128)(2,1)} async-done(((bf16[4,256,256]{1,2,0:T(8,128)(2,1)}), bf16[4,256,4096]{1,2,0:T(8,128)(2,1)}) %all-gather.7.cloned.1.call-update) | async-done | bytes 8388624 | tf_op jit(solution)/shard_map/all_gather | solution.py:30
  69.5 10.1 %fusion.2 = f32[2,256,4096]{2,1,0:T(8,128)} fusion(bf16[4,256,4096]{1,2,0:T(8,128)(2,1)} %all-gather.7.cloned.1.call-done, bf16[2,4]{1,0:T(2,128)(2,1)S(1)} %compare_convert_fusion, bf16[4,256,256]{1,2,0:T(8,128)(2,1)S(1)} %copy.43), kind=kOutput, calls=%fused_computation.3 | convolution fusion | flops 4295491584 | bytes 17301520 | tf_op jit(solution)/shard_map/pkr,kc->prc/dot_general | solution.py:32
  79.6 0.7 copy-done.2
  80.2 0.5 fusion.18
  80.8 0.3 fusion.16
  81.1 0.3 fusion.9
  81.3 1.1 constant_dynamic-slice_fusion.4
  82.5 16.4 %copy.46 = f32[2,256,256]{0,2,1:T(8,128)} copy(f32[2,256,256]{2,1,0:T(8,128)S(1)} %constant_dynamic-slice_fusion.4) | data formatting | bytes 1048576 | tf_op jit(solution)/shard_map/dynamic_slice | solution.py:33
  98.9 2.5 gather_fusion
  101.4 26.8 %all-reduce = (f32[2,256]{1,0:T(2,128)S(1)}, f32[2,256]{1,0:T(2,128)S(1)}) all-reduce(f32[2,256]{1,0:T(2,128)S(1)} %fusion.9, f32[2,256]{1,0:T(2,128)S(1)} %bitcast.136), channel_id=1, replica_groups=mesh['scen'=16,'blk'=16] {'scen'}, use_global_device_ids=true, to_apply=%region_0.1 | all-reduce | flops 1024 | bytes 8192 | tf_op jit(solution)/shard_map/psum | solution.py:40
  128.3 70.7 %all-gather = f32[256,16,2]{1,2,0:T(2,128)S(1)} all-gather(f32[1,16,2]{1,2,0:T(2,128)S(1)} %bitcast.132), channel_id=1, replica_groups=mesh['scen'=16,'blk'=16] {'scen','blk'}, dimensions={0}, use_global_device_ids=true | all-gather | bytes 32896 | tf_op jit(solution)/shard_map/all_gather | solution.py:55
  199.0 0.2 reshape.72
  199.4 0.1 reshape.100
  199.6 5.7 %copy.58 = f32[2,16,4096]{1,0,2:T(2,128)} copy(f32[2,16,4096]{2,1,0:T(8,128)} %reduce-scatter.2.cloned.1.call-done) | data formatting | bytes 1048576 | tf_op jit(solution)/shard_map/reduce_scatter | solution.py:43
  205.3 8.0 %reshape.107 = f32[16,1,8192]{2,1,0:T(1,128)} reshape(f32[4096,2,16]{2,1,0:T(2,128)} %bitcast.116) | data formatting | bytes 1048576
  213.2 6.8 %all-to-all-start = ((f32[16,1,8192]{2,1,0:T(1,128)}), f32[16,1,8192]{2,1,0:T(1,128)S(1)}, u32[]{:S(2)}, u32[]{:S(2)}) async-start(f32[16,1,8192]{2,1,0:T(1,128)} %reshape.107), calls=%async_computation.1 | async-start | bytes 1048576 | tf_op jit(solution)/shard_map/all_to_all | solution.py:44
  220.1 0.7 fusion.27
  220.8 61.2 %all-gather.1 = f32[256,16,2]{1,2,0:T(2,128)S(1)} all-gather(f32[1,16,2]{1,2,0:T(2,128)S(1)} %bitcast.134), channel_id=1, replica_groups=mesh['scen'=16,'blk'=16] {'scen','blk'}, dimensions={0}, use_global_device_ids=true | all-gather | bytes 32896 | tf_op jit(solution)/shard_map/all_gather | solution.py:55
  282.1 0.2 reshape.74
  282.5 0.1 reshape.102
  282.6 0.7 fusion.28
  283.4 59.3 %all-gather.2 = f32[256,16,2]{1,2,0:T(2,128)S(1)} all-gather(f32[1,16,2]{1,2,0:T(2,128)S(1)} %bitcast.135), channel_id=1, replica_groups=mesh['scen'=16,'blk'=16] {'scen','blk'}, dimensions={0}, use_global_device_ids=true | all-gather | bytes 32896 | tf_op jit(solution)/shard_map/all_gather | solution.py:55
  342.8 0.2 reshape.76
  342.9 0.1 reshape.59
  343.1 0.1 reshape.104
  343.3 0.7 fusion.29
  344.1 59.8 %all-gather.3 = f32[256,16,2]{1,2,0:T(2,128)S(1)} all-gather(f32[1,16,2]{1,2,0:T(2,128)S(1)} %bitcast.133), channel_id=1, replica_groups=mesh['scen'=16,'blk'=16] {'scen','blk'}, dimensions={0}, use_global_device_ids=true | all-gather | bytes 32896 | tf_op jit(solution)/shard_map/all_gather | solution.py:55
  403.9 0.2 reshape.78
  404.3 0.1 reshape.106
  404.5 0.7 fusion.30
  405.2 59.6 %all-gather.4 = f32[256,16,2]{1,2,0:T(2,128)S(1)} all-gather(f32[1,16,2]{1,2,0:T(2,128)S(1)} %add_bitcast_fusion), channel_id=1, replica_groups=mesh['scen'=16,'blk'=16] {'scen','blk'}, dimensions={0}, use_global_device_ids=true | all-gather | bytes 32896 | tf_op jit(solution)/shard_map/all_gather | solution.py:55
  464.8 0.2 reshape.80
  465.0 0.1 reshape.63
  465.2 0.2 reshape.64
  465.4 0.2 convolution_bitcast_fusion
  465.6 0.5 fusion.13
  466.1 23.1 %psum.23 = f32[4,256]{1,0:T(4,128)S(1)} all-reduce(f32[4,256]{1,0:T(4,128)S(1)} %bitcast.131), channel_id=1, replica_groups=mesh['scen'=16,'blk'=16] {'blk'}, use_global_device_ids=true, to_apply=%region_3.4 | all-reduce | flops 1024 | bytes 8192 | tf_op jit(solution)/shard_map/psum | solution.py:71
  489.2 0.5 fusion.11
  489.7 0.6 copy.103
  490.3 0.5 broadcast.39
  490.8 1.9 reduce
  492.7 6.9 %reshape.108 = f32[4096,2,16]{2,1,0:T(2,128)} reshape(f32[16,8192]{1,0:T(8,128)S(1)} %reduce) | data formatting | bytes 1048576
  499.6 6.3 %copy.59 = f32[2,16,16,256]{3,2,1,0:T(8,128)} copy(f32[2,16,16,256]{2,0,3,1:T(2,128)} %bitcast.115) | data formatting | bytes 1048576 | tf_op jit(solution)/shard_map/all_to_all | solution.py:44
  (43 shorter events, 1.6 us)
Async XLA Ops:
  7.2 1.9 copy-start
  7.2 62.3 %all-gather.7.cloned.1.call-start = ((), (), s32[]{:S(2)}) async-start(), calls=%async_computation.2 | async-start | bytes 8912896 | tf_op jit(solution)/shard_map/all_gather | solution.py:30
  10.3 189.3 %reduce-scatter.2.cloned.1.call-start = ((), (), s32[]{:S(2)}) async-start(), calls=%async_computation.3 | async-start | bytes 8912896 | tf_op jit(solution)/shard_map/reduce_scatter | solution.py:43
  79.6 0.7 copy-start.2
  79.6 1.5 copy-start.6
  82.4 45.8 %copy-start.3 = (f32[2,256]{1,0:T(2,128)S(1)}, f32[2,256]{1,0:T(2,128)}, u32[]{:S(2)}) copy-start(f32[2,256]{1,0:T(2,128)} %param.11) | copy-start | bytes 6148
  82.4 45.8 %copy-start.5 = (f32[2,256]{1,0:T(2,128)S(1)}, f32[2,256]{1,0:T(2,128)}, u32[]{:S(2)}) copy-start(f32[2,256]{1,0:T(2,128)} %param.10) | copy-start | bytes 6148
  199.6 20.5 %copy-start.1 = (f32[2,16,4096]{2,1,0:T(8,128)S(1)}, f32[2,16,4096]{2,1,0:T(8,128)}, u32[]{:S(2)}) copy-start(f32[2,16,4096]{2,1,0:T(8,128)} %reduce-scatter.2.cloned.1.call-done) | copy-start | bytes 1572868
  213.2 277.1 %all-to-all-start = ((f32[16,1,8192]{2,1,0:T(1,128)}), f32[16,1,8192]{2,1,0:T(1,128)S(1)}, u32[]{:S(2)}, u32[]{:S(2)}) async-start(f32[16,1,8192]{2,1,0:T(1,128)} %reshape.107), calls=%async_computation.1 | async-start | bytes 1048576 | tf_op jit(solution)/shard_map/all_to_all | solution.py:44
  465.4 40.5 %copy-start.4 = (f32[2,256]{1,0:T(2,128)}, f32[2,256]{1,0:T(2,128)S(1)}, u32[]{:S(2)}) copy-start(f32[2,256]{1,0:T(2,128)S(1)} %constant_dynamic-slice_fusion.1) | copy-start | bytes 6148
Sparse Core Ops, SparseCore 0:
  10.4 59.0 all-gather.6
  79.7 87.1 reduce-scatter.1
where the time goes:
time: 516 us; the launch traced here: 513 us
  blocking collectives  360 us (70%)
  waiting for transfers between devices  58.4 us (11%)
  local copies, waits for them, and re-layouts  51.6 us (10%)
  matrix products  16.2 us (3%)
  between operations  14.3 us (3%)
  starting transfers between devices  6.91 us (1%)
    all_gather x5, blocking collectives, assemble(): gathered = lax.all_gather(portion, ('scen', 'blk'), axis=1, tiled=True)  311 us
    all_gather x1, waiting for transfers between devices, body(): portion = lax.all_gather(solved, 'blk', axis=2, tiled=True)  58.3 us
    psum x1, blocking collectives, body(): rhs_sum, diag_sum = lax.psum((rhs_terms, diag_terms), 'scen')  26.8 us
    psum x1, blocking collectives, body(): summed = lax.psum(link_term, 'blk')  23.1 us
    dynamic_slice x2, local copies, waits for them, and re-layouts, body(): lax.dynamic_slice_in_dim(partial_value, blk_index * tile_width, tile_widt...  17.5 us
    unnamed x21, local copies, waits for them, and re-layouts  16.3 us
  transfers between devices with their start and end apart: 3, of which 1 were waited for; matrix products, arithmetic and copies ran while one was open for 6% of the time, Pallas kernels for 0%

commit v1 on v0

v1 whole, which is shorter than its diff:
```python
import functools

import jax
import jax.numpy as jnp
from jax import lax
from jax.experimental import pallas as pl
from jax.experimental.pallas import tpu as pltpu
from jax.sharding import PartitionSpec as P

ITERS = 4
DAMPING = 0.4
MESH = pl.DeviceIdType.MESH
F32 = jnp.float32
BF16 = jnp.bfloat16


def split_rows(v):
    hi = v.astype(BF16).astype(F32)
    rest = v - hi
    mid = rest.astype(BF16).astype(F32)
    low = rest - mid
    return jnp.concatenate([hi, mid, low, jnp.zeros_like(v)], axis=0).astype(BF16)


def leaf_products(v, mats_ref, contract):
    parts = split_rows(v)
    leaves = mats_ref.shape[0]
    row = lax.broadcasted_iota(jnp.int32, v.shape, 0)
    total = jnp.zeros(v.shape, F32)
    for leaf in range(leaves):
        out = lax.dot_general(
            parts, mats_ref[leaf], (((1,), (contract,)), ((), ())), preferred_element_type=F32
        )
        out = out[0:4] + out[4:8] + out[8:12]
        total = total + jnp.where(row == leaf, out, 0.0)
    return total


def solve_kernel(
    scens, blks,
    parent_ref, mask_ref, link_ref, inv_ref, rhs_ref, nrhs_ref, ndiag_ref,
    node_ref, leaf_ref,
    masked, solved, first, tbuf, ubuf, send_sem, recv_sem,
):
    scen = lax.axis_index("scen")
    blk = lax.axis_index("blk")
    leaves = link_ref.shape[0]
    barrier = pltpu.get_barrier_semaphore()
    for d in range(1, blks):
        pl.semaphore_signal(barrier, inc=1, device_id=(scen, lax.rem(blk + d, blks)), device_id_type=MESH)
    for d in range(1, scens):
        pl.semaphore_signal(barrier, inc=1, device_id=(lax.rem(scen + d, scens), blk), device_id_type=MESH)

    for leaf in range(leaves):
        m = link_ref[leaf] * mask_ref[leaf].astype(BF16)
        masked[leaf] = m
        solved[leaf] = jnp.dot(inv_ref[leaf], m, preferred_element_type=F32).astype(BF16)

    owner = [parent_ref[leaf].astype(F32) for leaf in range(leaves)]
    row2 = lax.broadcasted_iota(jnp.int32, nrhs_ref.shape, 0)
    row4 = lax.broadcasted_iota(jnp.int32, rhs_ref.shape, 0)

    def by_parent(rows):
        total = jnp.zeros(nrhs_ref.shape, F32)
        for leaf in range(leaves):
            weight = jnp.where(row2 == 0, 1.0 - owner[leaf], owner[leaf])
            total = total + weight * rows[leaf : leaf + 1]
        return total

    def of_parent(values):
        total = jnp.zeros(rhs_ref.shape, F32)
        for leaf in range(leaves):
            mine = values[0:1] * (1.0 - owner[leaf]) + values[1:2] * owner[leaf]
            total = total + jnp.where(row4 == leaf, mine, 0.0)
        return total

    def send(buf, index, value, over, me, count):
        buf[me] = value
        for d in range(1, count):
            peer = lax.rem(me + d, count)
            target = (scen, peer) if over == "blk" else (peer, blk)
            pltpu.make_async_remote_copy(
                src_ref=buf.at[me], dst_ref=buf.at[me],
                send_sem=send_sem.at[index], recv_sem=recv_sem.at[index],
                device_id=target, device_id_type=MESH,
            ).start()

    def collect(buf, index, count):
        rest = buf.at[pl.ds(0, count - 1)]
        pltpu.make_async_copy(rest, rest, recv_sem.at[index]).wait()
        total = buf[0]
        for j in range(1, count):
            total = total + buf[j]
        return total

    def drain(buf, index, count):
        rest = buf.at[pl.ds(0, count - 1)]
        pltpu.make_async_copy(rest, rest, send_sem.at[index]).wait()

    leaf_rhs = rhs_ref[...]
    leaf_solve = leaf_products(leaf_rhs, inv_ref, 1)
    rhs_terms = by_parent(leaf_products(leaf_solve, masked, 0))
    diag_rows = jnp.concatenate(
        [
            jnp.sum(masked[leaf].astype(F32) * solved[leaf].astype(F32), axis=0, keepdims=True)
            for leaf in range(leaves)
        ],
        axis=0,
    )
    diag_terms = by_parent(diag_rows)
    pl.semaphore_wait(barrier, (blks - 1) + (scens - 1))

    send(first, 0, jnp.concatenate([rhs_terms, diag_terms], axis=0), "scen", scen, scens)
    sums = collect(first, 0, scens)
    node_diag = ndiag_ref[...]
    reduced = nrhs_ref[...] - sums[0:2]
    scaling = node_diag + sums[2:4]
    x = reduced / scaling
    for it in range(ITERS):
        send(tbuf.at[it], 1 + it, leaf_products(of_parent(x), solved, 1), "blk", blk, blks)
        inner = collect(tbuf.at[it], 1 + it, blks)
        send(ubuf.at[it], 6 + it, by_parent(leaf_products(inner, masked, 0)), "scen", scen, scens)
        product = node_diag * x + collect(ubuf.at[it], 6 + it, scens)
        x = x + DAMPING * (reduced - product) / scaling
    node_ref[...] = x
    send(tbuf.at[ITERS], 1 + ITERS, leaf_products(of_parent(x), masked, 1), "blk", blk, blks)
    coupling = collect(tbuf.at[ITERS], 1 + ITERS, blks)
    leaf_ref[...] = leaf_products(leaf_rhs - coupling, inv_ref, 1)

    drain(first, 0, scens)
    for it in range(ITERS + 1):
        drain(tbuf.at[it], 1 + it, blks)
    for it in range(ITERS):
        drain(ubuf.at[it], 6 + it, scens)


def body(link, leaf_inverse, leaf_rhs, node_rhs, node_diag, parent, tile_mask):
    leaf_count, width_leaf, tile_width = link.shape
    node_count = node_rhs.shape[0]
    scens = lax.axis_size("scen")
    blks = lax.axis_size("blk")
    vmem = pl.BlockSpec(memory_space=pltpu.VMEM)
    smem = pl.BlockSpec(memory_space=pltpu.SMEM)
    node_solution, leaf_solution = pl.pallas_call(
        functools.partial(solve_kernel, scens, blks),
        out_shape=(
            jax.ShapeDtypeStruct((node_count, tile_width), F32),
            jax.ShapeDtypeStruct((leaf_count, width_leaf), F32),
        ),
        in_specs=[smem, smem] + [vmem] * 5,
        out_specs=(vmem, vmem),
        scratch_shapes=[
            pltpu.VMEM((leaf_count, width_leaf, tile_width), BF16),
            pltpu.VMEM((leaf_count, width_leaf, tile_width), BF16),
            pltpu.VMEM((scens, 2 * node_count, tile_width), F32),
            pltpu.VMEM((ITERS + 1, blks, leaf_count, width_leaf), F32),
            pltpu.VMEM((ITERS, scens, node_count, tile_width), F32),
            pltpu.SemaphoreType.DMA((10,)),
            pltpu.SemaphoreType.DMA((10,)),
        ],
        compiler_params=pltpu.CompilerParams(collective_id=0, has_side_effects=True),
        name="solve",
    )(parent, tile_mask.reshape(-1), link, leaf_inverse, leaf_rhs, node_rhs, node_diag)

    masked = link * tile_mask.astype(BF16)[:, :, None]
    solved = jnp.einsum("lnm,lmc->lnc", leaf_inverse, masked, preferred_element_type=F32).astype(BF16)
    node_ids = lax.broadcasted_iota(jnp.int32, (leaf_count, node_count), 1)
    member = (parent[:, None] == node_ids).astype(BF16)
    chosen = masked[None] * member.T[:, :, None, None]
    chosen = chosen.reshape(node_count, leaf_count * width_leaf, tile_width)
    stacked = lax.all_gather(solved.reshape(leaf_count * width_leaf, tile_width), "blk", axis=0)
    partial_value = jnp.einsum("pkr,skc->sprc", chosen, stacked, preferred_element_type=F32)
    schur_out = lax.psum_scatter(partial_value, "scen", scatter_dimension=0, tiled=False)
    return (node_solution, leaf_solution, schur_out)


def solution(mesh):
    in_specs = (
        P("scen", None, "blk"),
        P("scen", None, None),
        P("scen", None),
        P(None, "blk"),
        P(None, "blk"),
        P("scen"),
        P("scen", "blk"),
    )
    out_specs = (P(None, "blk"), P("scen", None), P(None, "blk", "scen"))
    return jax.shard_map(body, mesh=mesh, in_specs=in_specs, out_specs=out_specs, check_vma=False)
```

time: 516 us -> 183 us (0.35)
  blocking collectives: 360 us -> 0 us
  Pallas kernels: 0 us -> 56.6 us
  local copies, waits for them, and re-layouts: 51.6 us -> 4.59 us
  waiting for transfers between devices: 58.4 us -> 89.8 us
  starting transfers between devices: 6.91 us -> 0.08 us
    all_gather x5 -> x0, blocking collectives: 311 us -> none  [assemble(): gathered = lax.all_gather(portion, ('scen', 'blk'), axis=1, tiled=True)]
    pallas_call x0 -> x1, Pallas kernels: none -> 56.6 us  [body(): pl.pallas_call(functools.partial(solve_kernel, scens, blks), out_shape=(j...]
    psum x2 -> x0, blocking collectives: 49.8 us -> none  [the longest x1 26.8 us: body(): rhs_sum, diag_sum = lax.psum((rhs_terms, diag_terms), 'scen')]
    unnamed x2 -> x3, waiting for transfers between devices: 0.03 us -> 31.4 us
    dynamic_slice x3 -> x0, local copies, waits for them, and re-layouts: 17.5 us -> none  [the longest x2 17.5 us: body(): lax.dynamic_slice_in_dim(partial_value, blk_index * tile_width, tile_widt...]
    unnamed x21 -> x5, local copies, waits for them, and re-layouts: 16.3 us -> 4.59 us
    all_to_all x1 -> x0, starting transfers between devices: 6.83 us -> none  [body(): lax.all_to_all(schur_rows, 'scen', split_axis=2, concat_axis=1, tiled=True)]
    all_to_all x2 -> x0, local copies, waits for them, and re-layouts: 6.78 us -> none  [body(): lax.all_to_all(schur_rows, 'scen', split_axis=2, concat_axis=1, tiled=True)]
  transfers between devices with their start and end apart: 3 -> 2, of which waited for: 1 -> 2; matrix products, arithmetic and copies ran while one was open for 6% -> 0% of each run, Pallas kernels for 0% -> 31%
where the time goes in v1:
time: 183 us; the launch traced here: 181 us
  waiting for transfers between devices  89.8 us (49%)
  Pallas kernels  56.6 us (31%)
  between operations  14.1 us (8%)
  matrix products  13 us (7%)
  local copies, waits for them, and re-layouts  4.59 us (3%)
  other arithmetic  2.47 us (1%)
    all_gather x1, waiting for transfers between devices, body(): lax.all_gather(solved.reshape(leaf_count * width_leaf, tile_width), 'blk'...  58.4 us
    pallas_call x1, Pallas kernels, body(): pl.pallas_call(functools.partial(solve_kernel, scens, blks), out_shape=(j...  56.6 us
    unnamed x3, waiting for transfers between devices  31.4 us
    dot_general x1, matrix products, body(): jnp.einsum('pkr,skc->sprc', chosen, stacked, preferred_element_type=F32)  10.9 us
    unnamed x5, local copies, waits for them, and re-layouts  4.59 us
  transfers between devices with their start and end apart: 2, of which 2 were waited for; matrix products, arithmetic and copies ran while one was open for 0% of the time, Pallas kernels for 31%

profile of v1, /device:TPU:17, one launch (start us, length us, event | category | flops | bytes accessed | tf_op | source)
XLA Modules:
  0.0 180.6 jit_solution(12803848462422623732)
XLA Ops:
  7.2 0.0 all-gather.2.cloned.1.call-start
  7.2 0.7 convert_bitcast_fusion
  7.9 1.1 broadcast_multiply_fusion
  9.0 2.1 %convolution_convert_fusion = bf16[4,256,256]{1,2,0:T(8,128)(2,1)} fusion(bf16[4,256,256]{2,1,0:T(8,128)(2,1)} %inv_ref.1, bf16[4,256,256]{2,1,0:T(8,128)(2,1)S(1)} %broadcast_multiply_fusion), kind=kOutput, calls=%fused_computation.3 | convolution fusion | flops 134479872 | bytes 1572864 | tf_op jit(solution)/shard_map/lnm,lmc->lnc/dot_general | solution.py:166
  11.2 0.0 all-gather.2.cloned.1.call-update
  11.2 0.0 reduce-scatter.4.cloned.1.call-start
  11.2 0.7 compare_convert_fusion
  11.9 0.1 broadcast_bitcast_fusion
  12.0 58.4 %all-gather.2.cloned.1.call-done = bf16[16,1024,256]{2,1,0:T(8,128)(2,1)} async-done(((bf16[1,1024,256]{2,1,0:T(8,128)(2,1)}), bf16[16,1024,256]{2,1,0:T(8,128)(2,1)}) %all-gather.2.cloned.1.call-update) | async-done | bytes 8388624 | tf_op jit(solution)/shard_map/all_gather | solution.py:171
  70.4 10.9 %fusion.2 = f32[16,2,256,256]{2,3,1,0:T(8,128)} fusion(bf16[16,1024,256]{2,1,0:T(8,128)(2,1)} %all-gather.2.cloned.1.call-done, bf16[2,1024]{1,0:T(2,128)(2,1)S(1)} %bitcast.29, bf16[1024,256]{1,0:T(8,128)(2,1)S(1)} %bitcast.27), kind=kOutput, calls=%fused_computation.2 | convolution fusion | flops 4297064448 | bytes 17305600 | tf_op jit(solution)/shard_map/pkr,skc->sprc/dot_general | solution.py:172
  81.2 0.0 reduce-scatter.4.cloned.1.call-update
  81.3 56.6 %solve.1 = (f32[2,256]{1,0:T(2,128)}, f32[4,256]{1,0:T(4,128)}) custom-call(s32[4]{0:T(128)} %parent_ref.1, s32[4]{0:T(128)} %bitcast.30, bf16[4,256,256]{2,1,0:T(8,128)(2,1)} %link_ref.1, bf16[4,256,256]{2,1,0:T(8,128)(2,1)} %inv_ref.1, f32[4,256]{1,0:T(4,128)} %rhs_ref.1, f32[2,256]{1,0:T(2,128)} %nrhs_ref.1, f32[2,256]{1,0:T(2,128)} %ndiag_ref.1), custom_call_target="tpu_custom_call" | custom-call | tf_op jit(solution)/shard_map/solve/pallas_call | solution.py:144
  137.9 31.4 %reduce-scatter.4.cloned.1.call-done = f32[1,2,256,256]{2,3,1,0:T(8,128)} async-done(((f32[16,2,256,256]{2,3,1,0:T(8,128)}), f32[1,2,256,256]{2,3,1,0:T(8,128)}) %reduce-scatter.4.cloned.1.call-update) | async-done | bytes 524304
  169.2 2.0 %copy.13 = f32[2,256,256]{2,1,0:T(8,128)} copy(f32[2,256,256]{1,2,0:T(8,128)} %bitcast.28) | data formatting | bytes 1048576
  171.3 1.2 copy.20
  172.5 1.3 copy.21
  (1 shorter events, 0.0 us)
Async XLA Ops:
  7.2 63.2 %all-gather.2.cloned.1.call-start = ((), (), s32[]{:S(2)}) async-start(), calls=%async_computation.1 | async-start | bytes 8912896 | tf_op jit(solution)/shard_map/all_gather | solution.py:171
  11.2 158.1 %reduce-scatter.4.cloned.1.call-start = ((), (), s32[]{:S(2)}) async-start(), calls=%async_computation.2 | async-start | bytes 8912896
Sparse Core Ops, SparseCore 0:
  11.3 59.0 all-gather.1
  81.4 87.8 reduce-scatter.3
